TPU v7x, 32 devices: a whole 2x2x4 slice. The times are simulated.
32 devices in a mesh: group: 2 (over x), space: 16 (over z, y, core).
Axes of the slice: x: 2, y: 2, z: 4, core: 2. Of those that a mesh axis runs over, the one named last changes fastest.
Arguments:
- images: float32 [4, 128, 128, 128], P('group', 'space'), parts along dimension 0, may hold values from -2.7 to 2.7
- weights: float32 [4, 2], P('group'), parts along dimension 0, may hold values from 0 to 1
Outputs:
- relaxed: float32 [4, 128, 128, 128], P('group', 'space'), parts along dimension 0
- spacing: float32 [4, 1], P('group'), parts along dimension 0
There are 2 independent parts, one for each index of `group`. A program takes and returns all parts, laid end to end along the dimension named above; each array names one. Nothing has to cross between parts.
All inputs are finite; a program needn't handle non-finite values.
Results may differ from a plain program's by a relative error of at most 0.0002.
Values sent between devices are 32-bit elements; how exact they have to be, the bound alone decides.
No kernel may reach another device: no remote copies, remote signals or barrier semaphores. Data moves between devices by JAX's collectives and lax.ppermute only.
A program may use at most 64 MiB of HBM per device.

v0:
```python
import math

import jax
import jax.numpy as jnp
import numpy as np
from jax import lax
from jax.sharding import PartitionSpec as P

ITERS = 2

high = lax.Precision.HIGH
time_step = 0.1
gradient_weight = 1.0


def basis(length):
    index = np.arange(length)
    frequency = np.minimum(index, length - index)
    angles = (frequency[:, None] * index[None, :] % length) * (2.0 * math.pi / length)
    rows = np.where((index <= length // 2)[:, None], np.cos(angles), np.sin(angles))
    single = (frequency == 0) | (2 * frequency == length)
    scale = np.where(single, math.sqrt(1.0 / length), math.sqrt(2.0 / length))
    return (rows * scale[:, None]).astype(np.float32)


def wave_squares(length, indices):
    signed = jnp.where(indices <= length // 2, indices, indices - length)
    number = signed.astype(jnp.float32) * (2.0 * math.pi / length)
    return number * number


def local(images, weights):
    image_count, first_local, second_length, third_length = images.shape
    space_size = lax.axis_size("space")
    position = lax.axis_index("space")
    first_length = first_local * space_size
    second_local = second_length // space_size
    first = jnp.asarray(basis(first_length)).reshape(first_length, space_size, first_local)
    second = jnp.asarray(basis(second_length)).reshape(space_size, second_local, second_length)
    third = jnp.asarray(basis(third_length))
    local_rows = position * second_local + jnp.arange(second_local, dtype=jnp.int32)
    squares = (
        wave_squares(second_length, local_rows)[:, None, None]
        + wave_squares(first_length, jnp.arange(first_length, dtype=jnp.int32))[None, :, None]
        + wave_squares(third_length, jnp.arange(third_length, dtype=jnp.int32))[None, None, :]
    )
    damping = 1.0 / (1.0 + time_step * gradient_weight * squares * squares)
    coupling = time_step * squares * damping
    cell_count = first_length * second_length * third_length

    def forward(values):
        values = jnp.einsum("sby,fxyz->fxsbz", second, values, precision=high)
        values = jnp.einsum("fxsbz,kz->sfbxk", values, third, precision=high)
        values = lax.all_to_all(values, "space", 0, 0, tiled=True)
        return jnp.einsum("asx,sfbxk->fbak", first, values, precision=high)

    def backward(values, extra):
        values = jnp.einsum("asx,fbak->sfbxk", first, values, precision=high)
        sent = values.reshape(space_size, -1, third_length)
        if extra is not None:
            rows = jnp.broadcast_to(extra, (space_size,) + extra.shape)
            sent = jnp.concatenate([sent, rows], 1)
        sent = lax.all_to_all(sent, "space", 0, 0, tiled=True)
        count = values.size // (space_size * third_length)
        received = sent[:, :count].reshape(values.shape)
        values = jnp.einsum("sfbxk,kz->fxsbz", received, third, precision=high)
        values = jnp.einsum("sby,fxsbz->fxyz", second, values, precision=high)
        return values, sent[:, count:]

    concentration = images
    spectrum = None
    sums = []
    for iteration in range(ITERS):
        potential = concentration * concentration * concentration - concentration
        if iteration == 0:
            spectra = forward(jnp.concatenate([concentration, potential]))
            spectrum, potential = spectra[:image_count], spectra[image_count:]
        else:
            potential = forward(potential)
        spectrum = spectrum * damping - potential * coupling
        difference = spectrum[1:] - spectrum[:-1]
        sums.append(jnp.sum(difference * difference, axis=(1, 2, 3)))
        spectrum = jnp.einsum("ij,jbak->ibak", weights, spectrum, precision=lax.Precision.HIGHEST)
        extra = None
        if iteration == ITERS - 1:
            partial_sums = jnp.concatenate(sums)
            extra = jnp.pad(partial_sums[None], ((0, 7), (0, third_length - partial_sums.size)))
        concentration, extra = backward(spectrum, extra)
    totals = jnp.sum(extra[:, 0], axis=0)[: ITERS * (image_count - 1)] / cell_count
    return (concentration, totals.reshape(ITERS, image_count - 1))


def solution(mesh):
    placed = (P("group", "space", None, None), P("group", None))
    return jax.shard_map(
        local,
        mesh=mesh,
        in_specs=placed,
        out_specs=(P("group", "space", None, None), P("group", None)),
        check_vma=False,
    )
```

profile of v0, /device:TPU:0, one launch (start us, length us, event | category | flops | bytes accessed | tf_op | source)
XLA Modules:
  0.0 182.2 jit_solution(5724327323839884389)
XLA Ops:
  0.6 0.0 copy-start
  0.6 0.0 copy-start.3
  0.7 0.0 copy-start.1
  0.7 1.5 multiply_subtract_fusion.1
  2.1 0.1 copy-done.1
  2.2 1.0 fusion.10
  3.2 0.0 copy-done.4
  3.2 3.3 %fusion.7 = f32[16,4,8,8,128]{4,3,2,1,0:T(8,128)} fusion(f32[128,128,1,1,1]{1,0,4,2,3:T(8,128)S(1)} %copy-done.4, f32[4,8,16,8,128]{4,2,3,1,0:T(8,128)S(1)} %fusion.10), kind=kOutput, calls=%fused_computation.9 | convolution fusion | flops 402653184 | bytes 4259840 | tf_op jit(solution)/shard_map/fxsbz,kz->sfbxk/dot_general | solution.py:53
  6.6 7.5 %all-to-all-start = ((f32[16,4,8,8,128]{4,3,2,1,0:T(8,128)}), f32[16,4,8,8,128]{4,3,2,1,0:T(8,128)S(1)}, u32[]{:S(2)}, u32[]{:S(2)}) async-start(f32[16,4,8,8,128]{4,3,2,1,0:T(8,128)} %fusion.7), calls=%async_computation | async-start | bytes 4194304 | tf_op jit(solution)/shard_map/all_to_all | solution.py:54
  14.2 0.1 broadcast_add_fusion
  14.2 0.2 fusion.25
  14.4 40.7 %all-to-all-done = f32[16,4,8,8,128]{4,3,2,1,0:T(8,128)S(1)} async-done(((f32[16,4,8,8,128]{4,3,2,1,0:T(8,128)}), f32[16,4,8,8,128]{4,3,2,1,0:T(8,128)S(1)}, u32[]{:S(2)}, u32[]{:S(2)}) %all-to-all-start) | async-done | bytes 2097184 | tf_op jit(solution)/shard_map/all_to_all | solution.py:54
  55.1 0.0 copy-done.7
  55.1 1.8 %fusion.3 = f32[4,8,128,128,1]{3,2,0,1,4:T(8,128)S(1)} fusion(f32[128,16,8,1,1]{0,2,3,4,1:T(8,128)S(1)} %copy-done.7, f32[16,4,8,8,128]{4,3,2,1,0:T(8,128)S(1)} %all-to-all-done), kind=kOutput, calls=%fused_computation.5 | convolution fusion | flops 402653184 | bytes 4259840 | tf_op jit(solution)/shard_map/asx,sfbxk->fbak/dot_general | solution.py:55
  57.0 0.2 copy.97
  57.2 0.2 fusion.12
  57.4 0.0 copy-start.6
  57.4 1.3 copy.35
  58.7 4.9 %fusion.31 = f32[8,128,128,2]{2,3,1,0:T(2,128)S(1)} fusion(f32[2,8,128,128]{3,0,2,1:T(2,128)} %copy.35, f32[2,2]{1,0:T(2,128)S(1)} %copy-done), kind=kOutput, calls=%fused_computation.53 | convolution fusion | flops 6291456 | bytes 2097168 | tf_op jit(solution)/shard_map/ij,jbak->ibak/dot_general | solution.py:83
  63.7 0.0 copy-done.6
  63.7 0.6 fusion.13
  64.2 0.0 copy-start.5
  64.3 0.3 copy.39
  64.6 35.7 %all_to_all.20 = f32[16,128,128]{2,1,0:T(8,128)S(1)} all-to-all(f32[16,128,128]{2,1,0:T(8,128)S(1)} %copy.39), channel_id=1, replica_groups=mesh['group'=2,'space'=16] {'space'}, dimensions={0} | all-to-all | bytes 2097152 | tf_op jit(solution)/shard_map/all_to_all | solution.py:63
  100.3 1.1 convolution_bitcast_fusion.6
  101.4 1.0 fusion.11
  102.4 0.6 convolution_bitcast_fusion.4
  103.0 2.1 %convolution_bitcast_fusion.3 = f32[16,2,8,8,128]{4,3,2,1,0:T(8,128)} fusion(f32[128,128,1,1,1]{1,0,4,2,3:T(8,128)S(1)} %copy-done.4, f32[2,8,16,8,128]{4,2,3,1,0:T(8,128)S(1)} %convolution_bitcast_fusion.4), kind=kOutput, calls=%fused_computation.16 | convolution fusion | flops 201326592 | bytes 2162688 | tf_op jit(solution)/shard_map/fxsbz,kz->sfbxk/dot_general | solution.py:53
  105.1 5.1 %all-to-all-start.2 = ((f32[16,2,8,8,128]{4,3,2,1,0:T(8,128)}), f32[16,2,8,8,128]{4,3,2,1,0:T(8,128)}, u32[]{:S(2)}, u32[]{:S(2)}) async-start(f32[16,2,8,8,128]{4,3,2,1,0:T(8,128)} %convolution_bitcast_fusion.3), calls=%async_computation.2 | async-start | bytes 2097152 | tf_op jit(solution)/shard_map/all_to_all | solution.py:54
  110.1 1.3 copy.36
  111.4 0.7 fusion.29
  112.2 20.9 %all-to-all-done.2 = f32[16,2,8,8,128]{4,3,2,1,0:T(8,128)} async-done(((f32[16,2,8,8,128]{4,3,2,1,0:T(8,128)}), f32[16,2,8,8,128]{4,3,2,1,0:T(8,128)}, u32[]{:S(2)}, u32[]{:S(2)}) %all-to-all-start.2) | async-done | bytes 1048608 | tf_op jit(solution)/shard_map/all_to_all | solution.py:54
  133.1 2.2 %fusion.19 = f32[2,8,128,128,1]{3,2,0,1,4:T(8,128)S(1)} fusion(f32[128,16,8,1,1]{0,2,3,4,1:T(8,128)S(1)} %copy-done.7, f32[16,2,8,8,128]{4,3,2,1,0:T(8,128)} %all-to-all-done.2), kind=kOutput, calls=%fused_computation.33 | convolution fusion | flops 201326592 | bytes 2162688 | tf_op jit(solution)/shard_map/asx,sfbxk->fbak/dot_general | solution.py:55
  135.3 0.0 copy-done.2
  135.3 0.2 fusion.15
  135.5 0.7 fusion.27
  136.3 0.6 copy.43
  136.9 3.8 %convolution_bitcast_fusion = f32[2,8,128,128,1]{3,0,2,1,4:T(2,128)S(1)} fusion(f32[2,8,128,128]{3,0,2,1:T(2,128)S(1)} %copy.43, f32[2,2]{1,0:T(2,128)S(1)} %copy-done), kind=kOutput, calls=%fused_computation.13 | convolution fusion | flops 6291456 | bytes 2097168 | tf_op jit(solution)/shard_map/ij,jbak->ibak/dot_general | solution.py:83
  140.8 0.6 fusion.16
  141.3 0.3 copy.46
  141.7 1.3 maximum_bitcast_fusion.4
  143.0 0.1 pad_maximum_fusion
  143.1 35.1 %all_to_all.21 = f32[16,136,128]{2,1,0:T(8,128)S(1)} all-to-all(f32[16,136,128]{2,1,0:T(8,128)S(1)} %pad_maximum_fusion), channel_id=1, replica_groups=mesh['group'=2,'space'=16] {'space'}, dimensions={0} | all-to-all | bytes 2228224 | tf_op jit(solution)/shard_map/all_to_all | solution.py:63
  178.2 0.1 slice.44
  178.3 1.1 convolution_bitcast_fusion.2
  179.4 1.0 convolution_bitcast_fusion.1
  180.4 1.3 copy.48
  181.7 0.5 multiply_bitcast_fusion
  (11 shorter events, 0.1 us)
Async XLA Ops:
  0.6 58.1 %copy-start = (f32[2,2]{1,0:T(2,128)S(1)}, f32[2,2]{1,0:T(2,128)}, u32[]{:S(2)}) copy-start(f32[2,2]{1,0:T(2,128)} %param.6) | copy-start | bytes 52
  0.6 1.5 copy-start.3
  0.7 1.6 copy-start.1
  2.2 1.0 copy-start.4
  6.6 48.5 %copy-start.7 = (f32[128,16,8,1,1]{0,2,3,4,1:T(8,128)S(1)}, f32[128,16,8,1,1]{0,2,3,4,1:T(8,128)}, u32[]{:S(2)}) copy-start(f32[128,16,8,1,1]{0,2,3,4,1:T(8,128)} %constant.38) | copy-start | bytes 196612
  6.6 48.5 %all-to-all-start = ((f32[16,4,8,8,128]{4,3,2,1,0:T(8,128)}), f32[16,4,8,8,128]{4,3,2,1,0:T(8,128)S(1)}, u32[]{:S(2)}, u32[]{:S(2)}) async-start(f32[16,4,8,8,128]{4,3,2,1,0:T(8,128)} %fusion.7), calls=%async_computation | async-start | bytes 4194304 | tf_op jit(solution)/shard_map/all_to_all | solution.py:54
  57.4 6.3 %copy-start.6 = (f32[128,16,8,1,1]{0,1,2,4,3:T(8,128)S(1)}, f32[128,16,8,1,1]{0,1,2,4,3:T(8,128)}, u32[]{:S(2)}) copy-start(f32[128,16,8,1,1]{0,1,2,4,3:T(8,128)} %constant.40) | copy-start | bytes 196612
  64.2 36.1 %copy-start.5 = (f32[128,128,1,1,1]{1,0,3,4,2:T(8,128)S(1)}, f32[128,128,1,1,1]{1,0,3,4,2:T(8,128)}, u32[]{:S(2)}) copy-start(f32[128,128,1,1,1]{1,0,3,4,2:T(8,128)} %constant.41) | copy-start | bytes 196612
  105.1 28.0 %all-to-all-start.2 = ((f32[16,2,8,8,128]{4,3,2,1,0:T(8,128)}), f32[16,2,8,8,128]{4,3,2,1,0:T(8,128)}, u32[]{:S(2)}, u32[]{:S(2)}) async-start(f32[16,2,8,8,128]{4,3,2,1,0:T(8,128)} %convolution_bitcast_fusion.3), calls=%async_computation.2 | async-start | bytes 2097152 | tf_op jit(solution)/shard_map/all_to_all | solution.py:54
  112.2 23.1 %copy-start.2 = (f32[8,128,128,2]{1,2,0,3:T(8,128)S(1)}, f32[8,128,128,2]{1,2,0,3:T(8,128)}, u32[]{:S(2)}) copy-start(f32[8,128,128,2]{1,2,0,3:T(8,128)} %copy.36) | copy-start | bytes 3145732
where the time goes:
time: 183 us; the launch traced here: 182 us
  blocking collectives  70.8 us (39%)
  waiting for transfers between devices  61.5 us (34%)
  matrix products  25.1 us (14%)
  starting transfers between devices  12.6 us (7%)
  local copies, waits for them, and re-layouts  5.67 us (3%)
  other arithmetic  5.65 us (3%)
    all_to_all x2, blocking collectives, backward(): sent = lax.all_to_all(sent, 'space', 0, 0, tiled=True)  70.8 us
    all_to_all x2, waiting for transfers between devices, forward(): values = lax.all_to_all(values, 'space', 0, 0, tiled=True)  61.5 us
    all_to_all x2, starting transfers between devices, forward(): values = lax.all_to_all(values, 'space', 0, 0, tiled=True)  12.6 us
    dot_general x2, matrix products, local(): jnp.einsum('ij,jbak->ibak', weights, spectrum, precision=lax.Precision.HI...  8.77 us
    dot_general x2, matrix products, forward(): values = jnp.einsum('fxsbz,kz->sfbxk', values, third, precision=high)  5.42 us
    dot_general x2, matrix products, forward(): return jnp.einsum('asx,sfbxk->fbak', first, values, precision=high)  4.05 us
  transfers between devices with their start and end apart: 2, of which 2 were waited for; matrix products, arithmetic and copies ran while one was open for 1% of the time, Pallas kernels for 0%

commit v1 on v0

--- a/solution.py
+++ b/solution.py
@@ -1,9 +1,12 @@
+import functools
 import math
 
 import jax
 import jax.numpy as jnp
 import numpy as np
 from jax import lax
+from jax.experimental import pallas as pl
+from jax.experimental.pallas import tpu as pltpu
 from jax.sharding import PartitionSpec as P
 
 ITERS = 2
@@ -29,7 +32,243 @@
     return number * number
 
 
-def local(images, weights):
+def parts(matrix):
+    upper = matrix.astype(jnp.bfloat16)
+    return upper, (matrix - upper.astype(np.float32)).astype(jnp.bfloat16)
+
+
+def left_table(matrix):
+    upper, lower = parts(matrix)
+    return np.concatenate([upper, upper, lower], 1)
+
+
+def right_table(matrix):
+    upper, lower = parts(matrix)
+    return np.concatenate([upper, upper, lower], 0)
+
+
+def split(values):
+    upper = values.astype(jnp.bfloat16)
+    lower = (values - upper.astype(jnp.float32)).astype(jnp.bfloat16)
+    return upper, lower
+
+
+def from_left(table, values):
+    upper, lower = split(values)
+    return jnp.dot(table, jnp.concatenate([upper, lower, upper], 0), preferred_element_type=jnp.float32)
+
+
+def from_right(values, table):
+    upper, lower = split(values)
+    return jnp.dot(jnp.concatenate([upper, lower, upper], 1), table, preferred_element_type=jnp.float32)
+
+
+def potential_of(values):
+    return values * values * values - values
+
+
+def enter_spectrum(sizes, planes, second_table, third_table, scratch, send):
+    fields, space_size, first_local, second_local, second_length, third_length = sizes
+    for x in range(first_local):
+        mixed = from_left(second_table, planes(x))
+        for f in range(fields):
+            scratch[f, pl.ds(x * second_length, second_length), :] = mixed[:, f * third_length : (f + 1) * third_length]
+    count = second_local * first_local
+    for f in range(fields):
+        for d in range(space_size):
+            rows = [
+                scratch[f, pl.ds(d * second_local + b, first_local, stride=second_length), :]
+                for b in range(second_local)
+            ]
+            send[d, pl.ds(f * count, count), :] = from_right(jnp.concatenate(rows, 0), third_table)
+
+
+def leave_spectrum(sizes, received, third_table, second_table, scratch, put):
+    fields, space_size, first_local, second_local, second_length, third_length = sizes
+    count = second_local * first_local
+    for s in range(space_size):
+        scratch[pl.ds(s * fields * count, fields * count), :] = from_right(
+            received[s, pl.ds(0, fields * count), :], third_table
+        )
+    for x in range(first_local):
+        columns = []
+        for f in range(fields):
+            rows = [
+                scratch[pl.ds((s * fields + f) * count + x, second_local, stride=first_local), :]
+                for s in range(space_size)
+            ]
+            columns.append(jnp.concatenate(rows, 0))
+        put(x, from_left(second_table, jnp.concatenate(columns, 1)))
+
+
+def enter_kernel(sizes, images, second_table, third_table, send, scratch):
+    image_count = images.shape[0]
+
+    def planes(x):
+        values = jnp.concatenate([images[j, x] for j in range(image_count)], 1)
+        return jnp.concatenate([values, potential_of(values)], 1)
+
+    enter_spectrum(sizes, planes, second_table[...], third_table[...], scratch, send)
+
+
+def relax_kernel(sizes, first, last, refs):
+    image_count, space_size, first_local, second_local, second_length, third_length = sizes
+    if first:
+        weights, received, first_table, back_table, send, spectrum_out, sums_out = refs
+        fields = 2 * image_count
+    else:
+        weights, received, spectrum_in, sums_in, first_table, back_table, send = refs[:7]
+        if not last:
+            spectrum_out, sums_out = refs[7:]
+        fields = image_count
+    first_length = space_size * first_local
+    count = second_local * first_local
+    position = lax.axis_index("space")
+    shape = (first_length, third_length)
+    across = wave_squares(first_length, lax.broadcasted_iota(jnp.int32, shape, 0)) + wave_squares(
+        third_length, lax.broadcasted_iota(jnp.int32, shape, 1)
+    )
+    sums = [jnp.zeros((8, third_length), jnp.float32) for _ in range(image_count - 1)]
+    forward = first_table[...]
+    back = back_table[...]
+    for b in range(second_local):
+        columns = [
+            received[:, pl.ds(f * count + b * first_local, first_local), :].reshape(first_length, third_length)
+            for f in range(fields)
+        ]
+        spectra = from_left(forward, jnp.concatenate(columns, 1))
+        spectra = [spectra[:, f * third_length : (f + 1) * third_length] for f in range(fields)]
+        row = jnp.full((1, 1), position * second_local + b, jnp.int32)
+        squares = across + wave_squares(second_length, row)
+        damping = 1.0 / (1.0 + time_step * gradient_weight * squares * squares)
+        coupling = time_step * squares * damping
+        relaxed = []
+        for j in range(image_count):
+            field = spectra[j] if first else spectrum_in[b, j]
+            potential = spectra[image_count + j] if first else spectra[j]
+            relaxed.append(damping * field - coupling * potential)
+        for j in range(image_count - 1):
+            difference = relaxed[j + 1] - relaxed[j]
+            sums[j] = sums[j] + jnp.sum((difference * difference).reshape(-1, 8, third_length), axis=0)
+        mixed = []
+        for i in range(image_count):
+            total = weights[i, 0] * relaxed[0]
+            for j in range(1, image_count):
+                total = total + weights[i, j] * relaxed[j]
+            if not last:
+                spectrum_out[b, i] = total
+            mixed.append(total)
+        values = from_left(back, jnp.concatenate(mixed, 1))
+        for j in range(image_count):
+            send[:, pl.ds(j * count + b * first_local, first_local), :] = values[
+                :, j * third_length : (j + 1) * third_length
+            ].reshape(space_size, first_local, third_length)
+    own = jnp.concatenate([jnp.sum(total, axis=0, keepdims=True) for total in sums], 0)
+    if not first:
+        own = jnp.concatenate([sums_in[...], own], 0)
+    if last:
+        extra = send.shape[1] - image_count * count
+        own = jnp.concatenate([own, jnp.zeros((extra - own.shape[0], third_length), jnp.float32)], 0)
+        for d in range(space_size):
+            send[d, pl.ds(image_count * count, extra), :] = own
+    else:
+        sums_out[...] = own
+
+
+def turn_kernel(sizes, received, back_third, back_second, second_table, third_table, send, scratch, planes):
+    fields, space_size, first_local, second_local, second_length, third_length = sizes
+
+    def put(x, values):
+        planes[x] = potential_of(values)
+
+    leave_spectrum(sizes, received, back_third[...], back_second[...], scratch, put)
+    entering = scratch.reshape(fields, first_local * second_length, third_length)
+    enter_spectrum(sizes, lambda x: planes[x], second_table[...], third_table[...], entering, send)
+
+
+def leave_kernel(sizes, rows, cell_count, received, back_third, back_second, images, spacing, scratch):
+    fields, space_size, first_local, second_local, second_length, third_length = sizes
+
+    def put(x, values):
+        for j in range(fields):
+            images[j, x] = values[:, j * third_length : (j + 1) * third_length]
+
+    leave_spectrum(sizes, received, back_third[...], back_second[...], scratch, put)
+    count = fields * second_local * first_local
+    total = received[0, pl.ds(count, received.shape[1] - count), :]
+    for s in range(1, space_size):
+        total = total + received[s, pl.ds(count, received.shape[1] - count), :]
+    spacing[...] = jnp.sum(total, axis=1, keepdims=True)[:rows] / cell_count
+
+
+def call(kernel, outs, scratch, *args, smem=0):
+    space = [pl.BlockSpec(memory_space=pltpu.SMEM if i < smem else pltpu.VMEM) for i in range(len(args))]
+    return pl.pallas_call(
+        kernel,
+        out_shape=[jax.ShapeDtypeStruct(shape, jnp.float32) for shape in outs],
+        in_specs=space,
+        out_specs=[pl.BlockSpec(memory_space=pltpu.VMEM) for _ in outs],
+        scratch_shapes=[pltpu.VMEM(shape, jnp.float32) for shape in scratch],
+        compiler_params=pltpu.CompilerParams(vmem_limit_bytes=48 << 20),
+    )(*args)
+
+
+def exchange(values):
+    return lax.all_to_all(values, "space", 0, 0, tiled=True)
+
+
+def local_tiled(images, weights):
+    image_count, first_local, second_length, third_length = images.shape
+    space_size = lax.axis_size("space")
+    first_length = first_local * space_size
+    second_local = second_length // space_size
+    cell_count = first_length * second_length * third_length
+    first, second, third = basis(first_length), basis(second_length), basis(third_length)
+    enter_first, leave_first = left_table(first), left_table(first.T)
+    enter_second, leave_second = left_table(second), left_table(second.T)
+    enter_third, leave_third = right_table(third.T), right_table(third)
+    count = second_local * first_local
+    sizes = (space_size, first_local, second_local, second_length, third_length)
+    rows = ITERS * (image_count - 1)
+    extra = -(-rows // 8) * 8
+    plain = (space_size, image_count * count, third_length)
+    held = (space_size * image_count * count, third_length)
+    send = call(
+        functools.partial(enter_kernel, (2 * image_count,) + sizes),
+        [(space_size, 2 * image_count * count, third_length)],
+        [(2 * image_count, first_local * second_length, third_length)],
+        images, enter_second, enter_third,
+    )[0]
+    spectrum = sums = None
+    for iteration in range(ITERS):
+        received = exchange(send)
+        last = iteration == ITERS - 1
+        outs = [(space_size, image_count * count + (extra if last else 0), third_length)]
+        if not last:
+            outs.append((second_local, image_count, first_length, third_length))
+            outs.append(((iteration + 1) * (image_count - 1), third_length))
+        state = () if iteration == 0 else (spectrum, sums)
+        send, *state = call(
+            lambda *refs, first=iteration == 0, last=last: relax_kernel((image_count,) + sizes, first, last, refs),
+            outs, [], weights, received, *state, enter_first, leave_first, smem=1,
+        )
+        received = exchange(send)
+        if not last:
+            spectrum, sums = state
+            send = call(
+                functools.partial(turn_kernel, (image_count,) + sizes),
+                [plain], [held, (first_local, second_length, image_count * third_length)],
+                received, leave_third, leave_second, enter_second, enter_third,
+            )[0]
+    concentration, spacing = call(
+        functools.partial(leave_kernel, (image_count,) + sizes, rows, cell_count),
+        [images.shape, (rows, 1)], [held],
+        received, leave_third, leave_second,
+    )
+    return concentration, spacing.reshape(ITERS, image_count - 1)
+
+
+def local_plain(images, weights):
     image_count, first_local, second_length, third_length = images.shape
     space_size = lax.axis_size("space")
     position = lax.axis_index("space")
@@ -90,6 +329,13 @@
     return (concentration, totals.reshape(ITERS, image_count - 1))
 
 
+def local(images, weights):
+    first_local = images.shape[1]
+    second_local = images.shape[2] // lax.axis_size("space")
+    tiled = first_local % 8 == 0 and second_local % 8 == 0 and images.shape[3] % 128 == 0
+    return (local_tiled if tiled else local_plain)(images, weights)
+
+
 def solution(mesh):
     placed = (P("group", "space", None, None), P("group", None))
     return jax.shard_map(

time: 183 us -> 163 us (0.89)
  blocking collectives: 70.8 us -> 147 us
  waiting for transfers between devices: 61.5 us -> 0 us
  matrix products: 25.1 us -> 0 us
  starting transfers between devices: 12.6 us -> 0 us
  Pallas kernels: 0 us -> 11.2 us
  other arithmetic: 5.65 us -> 0 us
  local copies, waits for them, and re-layouts: 5.67 us -> 3.63 us
    all_to_all x2 -> x4, blocking collectives: 70.8 us -> 147 us  [exchange(): return lax.all_to_all(values, 'space', 0, 0, tiled=True)]
    all_to_all x2 -> x0, waiting for transfers between devices: 61.5 us -> none  [forward(): values = lax.all_to_all(values, 'space', 0, 0, tiled=True)]
    dot_general x14 -> x0, matrix products: 25.1 us -> none  [the longest x2 8.77 us: local(): jnp.einsum('ij,jbak->ibak', weights, spectrum, precision=lax.Precision.HI...]
    all_to_all x2 -> x0, starting transfers between devices: 12.6 us -> none  [forward(): values = lax.all_to_all(values, 'space', 0, 0, tiled=True)]
    pallas_call x0 -> x5, Pallas kernels: none -> 11.2 us  [call(): pl.pallas_call(kernel, out_shape=[jax.ShapeDtypeStruct(shape, jnp.float32...]
    sub x2 -> x0, local copies, waits for them, and re-layouts: 1.92 us -> none  [local(): spectrum = spectrum * damping - potential * coupling]
    sub x3 -> x0, other arithmetic: 1.9 us -> none  [the longest x1 1.45 us: local(): potential = concentration * concentration * concentration - concentration]
  transfers between devices with their start and end apart: 2 -> 0, of which waited for: 2 -> 0; matrix products, arithmetic and copies ran while one was open for 1% -> 0% of each run, Pallas kernels for 0% -> 0%
where the time goes in v1:
time: 163 us; the launch traced here: 162 us
  blocking collectives  147 us (90%)
  Pallas kernels  11.2 us (7%)
  local copies, waits for them, and re-layouts  3.63 us (2%)
    all_to_all x4, blocking collectives, exchange(): return lax.all_to_all(values, 'space', 0, 0, tiled=True)  147 us
    pallas_call x5, Pallas kernels, call(): pl.pallas_call(kernel, out_shape=[jax.ShapeDtypeStruct(shape, jnp.float32...  11.2 us

profile of v1, /device:TPU:0, one launch (start us, length us, event | category | flops | bytes accessed | tf_op | source)
XLA Modules:
  0.0 162.4 jit_solution(17010124508629297430)
XLA Ops:
  0.6 0.0 copy-start
  0.6 0.9 copy-done
  1.5 0.0 copy-start.3
  1.5 1.2 copy-done.3
  2.8 0.0 copy-start.4
  2.8 0.9 copy-done.4
  3.6 2.2 %shard_map.95 = f32[16,256,128]{2,1,0:T(8,128)S(1)} custom-call(f32[2,8,128,128]{3,2,1,0:T(8,128)S(1)} %copy-done.3, bf16[128,384]{1,0:T(8,128)(2,1)S(1)} %copy-done, bf16[384,128]{1,0:T(8,128)(2,1)S(1)} %copy-done.4), custom_call_target="tpu_custom_call" | custom-call | tf_op jit(solution)/shard_map/pallas_call | solution.py:206
  5.9 0.0 copy-start.1
  5.9 0.0 copy-start.2
  5.9 0.0 copy-start.7
  5.9 54.5 %all_to_all.20.refs_1_ = f32[16,256,128]{2,1,0:T(8,128)S(1)} all-to-all(f32[16,256,128]{2,1,0:T(8,128)S(1)} %shard_map.95), channel_id=1, replica_groups=mesh['group'=2,'space'=16] {'space'}, dimensions={0} | all-to-all | bytes 4194304 | tf_op jit(solution)/shard_map/all_to_all | solution.py:217
  60.4 0.0 copy-done.1
  60.4 0.0 copy-done.2
  60.4 0.0 copy-done.7
  60.4 0.0 copy-start.5
  60.4 0.0 copy-start.6
  60.4 3.1 %shard_map.96 = (f32[16,128,128]{2,1,0:T(8,128)S(1)}, f32[8,2,128,128]{3,2,1,0:T(8,128)S(1)}, f32[1,128]{1,0:T(1,128)S(1)}) custom-call(f32[2,2]{1,0:T(2,128)S(1)} %copy-done.7, f32[16,256,128]{2,1,0:T(8,128)S(1)} %all_to_all.20.refs_1_, bf16[128,384]{1,0:T(8,128)(2,1)S(1)} %copy-done.1, bf16[128,384]{1,0:T(8,128)(2,1)S(1)} %copy-done.2), custom_call_target="tpu_custom_call" | custom-call | tf_op jit(solution)/shard_map/pallas_call | solution.py:206
  63.5 29.6 %all_to_all.21.received = f32[16,128,128]{2,1,0:T(8,128)S(1)} all-to-all(f32[16,128,128]{2,1,0:T(8,128)S(1)} %get-tuple-element.5), channel_id=1, replica_groups=mesh['group'=2,'space'=16] {'space'}, dimensions={0} | all-to-all | bytes 2097152 | tf_op jit(solution)/shard_map/all_to_all | solution.py:217
  93.2 0.0 copy-done.5
  93.2 0.0 copy-done.6
  93.2 2.2 %shard_map.97 = f32[16,128,128]{2,1,0:T(8,128)S(1)} custom-call(f32[16,128,128]{2,1,0:T(8,128)S(1)} %all_to_all.21.received, bf16[384,128]{1,0:T(8,128)(2,1)S(1)} %copy-done.6, bf16[128,384]{1,0:T(8,128)(2,1)S(1)} %copy-done.2, bf16[128,384]{1,0:T(8,128)(2,1)S(1)} %copy-done.1, bf16[384,128]{1,0:T(8,128)(2,1)S(1)} %copy-done.5), custom_call_target="tpu_custom_call" | custom-call | tf_op jit(solution)/shard_map/pallas_call | solution.py:206
  95.4 29.5 %all_to_all.22.refs_1_ = f32[16,128,128]{2,1,0:T(8,128)S(1)} all-to-all(f32[16,128,128]{2,1,0:T(8,128)S(1)} %shard_map.97), channel_id=1, replica_groups=mesh['group'=2,'space'=16] {'space'}, dimensions={0} | all-to-all | bytes 2097152 | tf_op jit(solution)/shard_map/all_to_all | solution.py:217
  124.9 1.6 shard_map.98
  126.5 33.3 %all_to_all.23.received = f32[16,136,128]{2,1,0:T(8,128)S(1)} all-to-all(f32[16,136,128]{2,1,0:T(8,128)S(1)} %shard_map.98), channel_id=1, replica_groups=mesh['group'=2,'space'=16] {'space'}, dimensions={0} | all-to-all | bytes 2228224 | tf_op jit(solution)/shard_map/all_to_all | solution.py:217
  159.8 2.1 %shard_map.99 = (f32[2,8,128,128]{3,2,1,0:T(8,128)}, f32[2,1]{1,0:T(2,128)S(1)}) custom-call(f32[16,136,128]{2,1,0:T(8,128)S(1)} %all_to_all.23.received, bf16[384,128]{1,0:T(8,128)(2,1)S(1)} %copy-done.6, bf16[128,384]{1,0:T(8,128)(2,1)S(1)} %copy-done.2), custom_call_target="tpu_custom_call" | custom-call | tf_op jit(solution)/shard_map/pallas_call | solution.py:206
  161.8 0.6 copy.10
Async XLA Ops:
  0.6 0.9 copy-start
  1.5 1.2 copy-start.3
  2.8 0.9 copy-start.4
  5.9 54.5 %copy-start.1 = (bf16[128,384]{1,0:T(8,128)(2,1)S(1)}, bf16[128,384]{1,0:T(8,128)(2,1)}, u32[]{:S(2)}) copy-start(bf16[128,384]{1,0:T(8,128)(2,1)} %constant.8.clone.second_table.refs_2_.refs_4_) | copy-start | bytes 294916
  5.9 54.5 %copy-start.2 = (bf16[128,384]{1,0:T(8,128)(2,1)S(1)}, bf16[128,384]{1,0:T(8,128)(2,1)}, u32[]{:S(2)}) copy-start(bf16[128,384]{1,0:T(8,128)(2,1)} %constant.10.clone.refs_3_.back_second.refs_5_) | copy-start | bytes 294916
  5.9 54.5 %copy-start.7 = (f32[2,2]{1,0:T(2,128)S(1)}, f32[2,2]{1,0:T(2,128)}, u32[]{:S(2)}) copy-start(f32[2,2]{1,0:T(2,128)} %refs_0_.3) | copy-start | bytes 52
  60.4 32.8 %copy-start.5 = (bf16[384,128]{1,0:T(8,128)(2,1)S(1)}, bf16[384,128]{1,0:T(8,128)(2,1)}, u32[]{:S(2)}) copy-start(bf16[384,128]{1,0:T(8,128)(2,1)} %constant.9.clone.third_table) | copy-start | bytes 294916
  60.4 32.8 %copy-start.6 = (bf16[384,128]{1,0:T(8,128)(2,1)S(1)}, bf16[384,128]{1,0:T(8,128)(2,1)}, u32[]{:S(2)}) copy-start(bf16[384,128]{1,0:T(8,128)(2,1)} %constant.11.clone.back_third) | copy-start | bytes 294916
